TPU v7x, 128 devices: a whole 4x4x4 slice. The times are simulated.
128 devices in a mesh: resp: 32 (over x, z, y_lo), head: 4 (over y_hi, core).
Axes of the slice: x: 4, y: 4 (y_hi: 2, y_lo: 2; y = y_hi * 2 + y_lo), z: 4, core: 2. Of those that a mesh axis runs over, the one named last changes fastest.
Arguments:
- queries: bfloat16 [32, 512, 5120], P('resp', None, 'head'), may hold values from -8 to 8
- resp_keys: bfloat16 [32, 512, 1024], P('resp', None, 'head'), may hold values from -6 to 6
- resp_values: bfloat16 [32, 512, 1024], P('resp', None, 'head'), may hold values from -6 to 6
- prompt_keys: bfloat16 [1024, 1024], P(('resp', 'head')), may hold values from -8 to 8
- prompt_values: bfloat16 [1024, 1024], P(('resp', 'head')), may hold values from -6 to 6
- lengths: int32 [32], P('resp'), may hold values from 64 to 512, as said below
- loss_mask: int32 [32, 512], P('resp'), may hold values 0 or 1
- out_grad: bfloat16 [32, 512, 5120], P('resp', None, 'head'), may hold values from -6 to 6
Outputs:
- attended: bfloat16 [32, 512, 5120], P('resp', None, 'head')
- query_grad: bfloat16 [32, 512, 5120], P('resp', None, 'head')
- key_grad: bfloat16 [32, 512, 1024], P('resp', None, 'head')
- value_grad: bfloat16 [32, 512, 1024], P('resp', None, 'head')
- prompt_key_grad: float32 [1024, 1024], P(('resp', 'head'))
- prompt_value_grad: float32 [1024, 1024], P(('resp', 'head'))
Inputs may be any that keep to these rules, and one draw needn't show every extreme that they name: `lengths`: the longest response has exactly 512 live positions.
All inputs are finite; a program needn't handle non-finite values. No bound on the sum of `loss_mask` on one device may be relied on, other than what follows from the above.
Results may differ from a plain program's by a relative error of at most 0.035.
Values may be sent and summed in bfloat16 or wider, within the bound.
A program may use at most 128 MiB of HBM per device.

v0:
```python
import jax
import jax.numpy as jnp
from jax import lax
from jax.sharding import PartitionSpec as P

HEAD_DIM = 128


def respond(
    query_row, key_row, value_row, length, keep_row, grad_row, prompt_key3, prompt_value3, kv_count
):
    steps_len = query_row.shape[0]
    group_size = query_row.shape[1] // (kv_count * HEAD_DIM)
    score_scale = HEAD_DIM ** (-0.5)
    positions = jnp.arange(steps_len)
    query_five = query_row.reshape(steps_len, kv_count, group_size, HEAD_DIM)
    own_key = key_row.reshape(steps_len, kv_count, HEAD_DIM)
    own_value = value_row.reshape(steps_len, kv_count, HEAD_DIM)
    prompt_scores = (
        jnp.einsum("tkgd,jkd->kgtj", query_five, prompt_key3, preferred_element_type=jnp.float32)
        * score_scale
    )
    own_scores = (
        jnp.einsum("tkgd,jkd->kgtj", query_five, own_key, preferred_element_type=jnp.float32)
        * score_scale
    )
    allowed = (positions[None, :] <= positions[:, None]) & (positions[None, :] < length)
    own_scores = jnp.where(allowed, own_scores, -jnp.inf)
    row_top = jnp.maximum(prompt_scores.max(-1), own_scores.max(-1))
    row_total = jnp.exp(prompt_scores - row_top[..., None]).sum(-1) + jnp.exp(
        own_scores - row_top[..., None]
    ).sum(-1)
    log_total = row_top + jnp.log(row_total)
    prompt_prob = jnp.exp(prompt_scores - log_total[..., None])
    own_prob = jnp.exp(own_scores - log_total[..., None])
    prompt_weight = prompt_prob.astype(jnp.bfloat16)
    own_weight = own_prob.astype(jnp.bfloat16)
    live_rows = positions < length
    attended = jnp.einsum(
        "kgtj,jkd->tkgd", prompt_weight, prompt_value3, preferred_element_type=jnp.float32
    ) + jnp.einsum("kgtj,jkd->tkgd", own_weight, own_value, preferred_element_type=jnp.float32)
    attended = jnp.where(live_rows[:, None, None, None], attended, 0.0).astype(jnp.bfloat16)
    grad_factor = (keep_row * live_rows.astype(jnp.int32)).astype(jnp.bfloat16)
    grad_five = (
        grad_row.reshape(steps_len, kv_count, group_size, HEAD_DIM)
        * grad_factor[:, None, None, None]
    )
    row_delta = jnp.einsum(
        "tkgd,tkgd->kgt", grad_five, attended, preferred_element_type=jnp.float32
    )
    prompt_dprob = jnp.einsum(
        "tkgd,jkd->kgtj", grad_five, prompt_value3, preferred_element_type=jnp.float32
    )
    own_dprob = jnp.einsum(
        "tkgd,jkd->kgtj", grad_five, own_value, preferred_element_type=jnp.float32
    )
    prompt_ds = (prompt_prob * (prompt_dprob - row_delta[..., None]) * score_scale).astype(
        jnp.bfloat16
    )
    own_ds = (own_prob * (own_dprob - row_delta[..., None]) * score_scale).astype(jnp.bfloat16)
    query_grad = jnp.einsum(
        "kgtj,jkd->tkgd", prompt_ds, prompt_key3, preferred_element_type=jnp.float32
    ) + jnp.einsum("kgtj,jkd->tkgd", own_ds, own_key, preferred_element_type=jnp.float32)
    key_grad = jnp.einsum("kgtj,tkgd->jkd", own_ds, query_five, preferred_element_type=jnp.float32)
    value_grad = jnp.einsum(
        "kgtj,tkgd->jkd", own_weight, grad_five, preferred_element_type=jnp.float32
    )
    return (
        attended.reshape(query_row.shape),
        query_grad.astype(jnp.bfloat16).reshape(query_row.shape),
        key_grad.astype(jnp.bfloat16).reshape(key_row.shape),
        value_grad.astype(jnp.bfloat16).reshape(key_row.shape),
        prompt_ds,
        prompt_weight,
        grad_five,
    )


def per_device(
    queries, resp_keys, resp_values, prompt_keys, prompt_values, lengths, loss_mask, out_grad
):
    kv_width = resp_keys.shape[2]
    kv_count = kv_width // HEAD_DIM
    every_key, every_value = (
        lax.all_gather(prompt_keys, ("resp", "head"), axis=0, tiled=True),
        lax.all_gather(prompt_values, ("resp", "head"), axis=0, tiled=True),
    )
    head_start = lax.axis_index("head") * kv_width
    group_keys = lax.dynamic_slice_in_dim(every_key, head_start, kv_width, 1)
    group_values = lax.dynamic_slice_in_dim(every_value, head_start, kv_width, 1)
    prompt_rows = group_keys.shape[0]
    prompt_key3 = group_keys.reshape(prompt_rows, kv_count, HEAD_DIM)
    prompt_value3 = group_values.reshape(prompt_rows, kv_count, HEAD_DIM)

    def one_response(inputs):
        query_row, key_row, value_row, length, keep_row, grad_row = inputs
        return respond(
            query_row,
            key_row,
            value_row,
            length,
            keep_row,
            grad_row,
            prompt_key3,
            prompt_value3,
            kv_count,
        )

    results = lax.map(one_response, (queries, resp_keys, resp_values, lengths, loss_mask, out_grad))
    attended, query_grad, key_grad, value_grad, prompt_ds, prompt_weight, grad_all = results
    query_all = queries.reshape(queries.shape[0], queries.shape[1], kv_count, -1, HEAD_DIM)
    local_rows = prompt_rows // lax.axis_size("resp")
    key_part = jnp.einsum(
        "rkgtj,rtkgd->jkd", prompt_ds, query_all, preferred_element_type=jnp.float32
    )
    value_part = jnp.einsum(
        "rkgtj,rtkgd->jkd", prompt_weight, grad_all, preferred_element_type=jnp.float32
    )
    whole_sum = lax.psum(
        jnp.concatenate(
            [key_part.reshape(prompt_rows, kv_width), value_part.reshape(prompt_rows, kv_width)], 1
        ),
        "resp",
    )
    summed = lax.dynamic_slice_in_dim(whole_sum, lax.axis_index("resp") * local_rows, local_rows, 0)
    key_sum = summed[:, :kv_width]
    value_sum = summed[:, kv_width:]
    prompt_key_grad, prompt_value_grad = (
        lax.all_to_all(key_sum, "head", split_axis=0, concat_axis=1, tiled=True),
        lax.all_to_all(value_sum, "head", split_axis=0, concat_axis=1, tiled=True),
    )
    return (attended, query_grad, key_grad, value_grad, prompt_key_grad, prompt_value_grad)


def solution(mesh):
    placed = (
        P("resp", None, "head"),
        P("resp", None, "head"),
        P("resp", None, "head"),
        P(("resp", "head"), None),
        P(("resp", "head"), None),
        P("resp"),
        P("resp", None),
        P("resp", None, "head"),
    )
    return jax.shard_map(
        per_device,
        mesh=mesh,
        in_specs=placed,
        out_specs=(
            P("resp", None, "head"),
            P("resp", None, "head"),
            P("resp", None, "head"),
            P("resp", None, "head"),
            P(("resp", "head"), None),
            P(("resp", "head"), None),
        ),
        check_vma=False,
    )
```

profile of v0, /device:TPU:1, one launch (start us, length us, event | category | flops | bytes accessed | tf_op | source)
XLA Modules:
  0.0 827.9 jit_solution(10407376835702045725)
XLA Ops:
  8.7 1.6 copy.74
  11.0 1.0 reshape.109
  12.2 2.5 copy.82
  14.7 1.7 reshape.110
  17.3 6.3 fusion.11
  23.6 183.4 %all-gather.3.cloned.1.call-done = bf16[1024,1024]{1,0:T(8,128)(2,1)} async-done(((bf16[8,1024]{1,0:T(8,128)(2,1)}), bf16[1024,1024]{1,0:T(8,128)(2,1)}) %all-gather.3.cloned.1.call-update) | async-done | bytes 2097168 | tf_op jit(solution)/shard_map/all_gather | solution.py:86
  207.0 194.5 %all-gather.5.cloned.1.call-done = bf16[1024,1024]{1,0:T(8,128)(2,1)} async-done(((bf16[8,1024]{1,0:T(8,128)(2,1)}), bf16[1024,1024]{1,0:T(8,128)(2,1)}) %all-gather.5.cloned.1.call-update) | async-done | bytes 2097168 | tf_op jit(solution)/shard_map/all_gather | solution.py:85
  401.5 2.1 constant_dynamic-slice_fusion
  403.6 1.0 copy.145
  404.6 4.0 bitcast_reduce_fusion
  408.6 14.2 %exponential_reduce_fusion = f32[2,5,512]{2,1,0:T(8,128)} fusion(f32[2,512,512,5]{2,1,3,0:T(8,128)} %get-tuple-element.77, f32[2,5,512]{2,1,0:T(8,128)S(1)} %max.11, pred[512,512]{0,1:T(8,128)(4,1)S(1)} %fusion.22), kind=kLoop, calls=%fused_computation.17 | loop fusion | flops 10480640 | bytes 10788864 | tf_op jit(solution)/shard_map/while/body/eval_jaxpr/reduce_sum | solution.py:32
  422.8 3.7 fusion.4
  426.5 12.4 %fusion.16 = f32[2,128,1024,1]{2,1,3,0:T(8,128)} fusion(f32[2,1024,512,5]{2,1,3,0:T(8,128)} %copy-done, f32[2,5,512]{2,1,0:T(8,128)S(1)} %log_add_fusion, bf16[512,2,5,128]{0,3,2,1:T(8,128)(2,1)} %bitcast.152, bf16[512]{0:T(512)(128)(2,1)S(1)} %select_convert_fusion), kind=kOutput, calls=%fused_computation.28 | convolution fusion | flops 1358561280 | bytes 23352320 | tf_op jit(solution)/shard_map/rkgtj,rtkgd->jkd/dot_general | solution.py:116
  439.0 2.7 copy.96
  441.7 2.0 copy.72
  443.7 9.3 %fusion.18 = f32[2,128,5,512]{3,1,2,0:T(8,128)S(1)} fusion(bf16[1024,2,128,1]{0,2,3,1:T(8,128)(2,1)} %bitcast.162, f32[2,1024,512,5]{2,1,3,0:T(8,128)} %copy-done, f32[2,5,512]{2,1,0:T(8,128)S(1)} %log_add_fusion), kind=kOutput, calls=%fused_computation.29 | convolution fusion | flops 1357905920 | bytes 24137728 | tf_op jit(solution)/shard_map/while/body/eval_jaxpr/kgtj,jkd->tkgd/dot_general | solution.py:39
  453.7 4.2 fusion.13
  457.8 13.0 %fusion.2 = bf16[2,5,512,1024]{2,3,1,0:T(8,128)(2,1)} fusion(f32[2,1024,512,5]{2,1,3,0:T(8,128)} %copy-done, f32[2,5,512]{2,1,0:T(8,128)S(1)} %get-tuple-element.78, f32[2,5,512]{2,1,0:T(8,128)S(1)} %log_add_fusion, bf16[1024,2,128,1]{0,2,3,1:T(8,128)(2,1)} %bitcast.163, bf16[512,2,5,128]{0,3,2,1:T(8,128)(2,1)} %bitcast.153, ...), kind=kOutput, calls=%fused_computation.3 | convolution fusion | flops 1376256000 | bytes 33334272 | tf_op jit(solution)/shard_map/while/body/eval_jaxpr/tkgd,jkd->kgtj/dot_general | solution.py:51
  470.8 7.5 fusion.38
  478.3 1.3 copy.95
  479.6 3.3 pad_maximum_fusion
  483.0 7.2 fusion.37
  490.1 7.5 fusion.21
  497.7 5.2 fusion.9
  503.0 270.5 %all-reduce.2.cloned.1.call-done = f32[1024,512]{1,0:T(8,128)} async-done(((f32[1024,512]{1,0:T(8,128)}), f32[1024,512]{1,0:T(8,128)}) %all-reduce.2.cloned.1.call-update) | async-done | bytes 2097168 | tf_op jit(solution)/shard_map/psum | solution.py:119
  773.4 1.4 dynamic-slice_bitcast_fusion
  774.8 26.5 %all-to-all-start = ((f32[4,8,256]{2,1,0:T(8,128)}), f32[4,8,256]{2,1,0:T(8,128)S(1)}, u32[]{:S(2)}, u32[]{:S(2)}) async-start(f32[4,8,256]{2,1,0:T(8,128)} %get-tuple-element.73), calls=%async_computation | async-start | bytes 65536 | tf_op jit(solution)/shard_map/all_to_all | solution.py:129
  801.3 4.2 fusion.12
  806.0 4.3 all-to-all-start.1
  810.3 4.3 fusion.20
  814.6 1.4 copy.98
  817.7 2.4 copy.97
  (60 shorter events, 6.6 us)
Async XLA Ops:
  7.2 199.8 %all-gather.3.cloned.1.call-start = ((), (), s32[]{:S(2)}) async-start(), calls=%async_computation.2 | async-start | bytes 2113536 | tf_op jit(solution)/shard_map/all_gather | solution.py:86
  7.9 393.6 %all-gather.5.cloned.1.call-start = ((), (), s32[]{:S(2)}) async-start(), calls=%async_computation.3 | async-start | bytes 2113536 | tf_op jit(solution)/shard_map/all_gather | solution.py:85
  8.6 764.8 %all-reduce.2.cloned.1.call-start = ((), (), s32[]{:S(2)}) async-start(), calls=%async_computation.4 | async-start | bytes 4194304 | tf_op jit(solution)/shard_map/psum | solution.py:119
  12.2 392.4 %copy-start.7 = (bf16[512,2,128,1]{0,2,3,1:T(8,128)(2,1)}, bf16[512,2,128,1]{0,2,3,1:T(8,128)(2,1)S(1)}, u32[]{:S(2)}) copy-start(bf16[512,2,128,1]{0,2,3,1:T(8,128)(2,1)S(1)} %copy.123) | copy-start | bytes 786436
  17.2 391.4 %copy-start.4 = (pred[512,512]{0,1:T(8,128)(4,1)}, pred[512,512]{0,1:T(8,128)(4,1)S(1)}, u32[]{:S(2)}) copy-start(pred[512,512]{0,1:T(8,128)(4,1)S(1)} %fusion.22) | copy-start | bytes 786436
  404.6 4.0 copy-start.12
  408.6 17.9 %copy-start = (f32[2,1024,512,5]{2,1,3,0:T(8,128)}, f32[2,1024,512,5]{2,1,3,0:T(8,128)S(1)}, u32[]{:S(2)}) copy-start(f32[2,1024,512,5]{2,1,3,0:T(8,128)S(1)} %get-tuple-element.75) | copy-start | bytes 62914564
  422.8 3.7 copy-start.13
  439.0 14.1 %slice-start = ((s8[10485760]{0:T(1024)(128)(4,1)}), s8[2097152]{0:T(1024)(128)(4,1)S(1)}, s32[]{:S(2)}) async-start(s8[10485760]{0:T(1024)(128)(4,1)} %bitcast.144), calls=%async_computation.5 | async-start | bytes 4194304
  443.7 9.4 %slice-start.1 = ((s8[10485760]{0:T(1024)(128)(4,1)}), s8[4194304]{0:T(1024)(128)(4,1)S(1)}, s32[]{:S(2)}) async-start(s8[10485760]{0:T(1024)(128)(4,1)} %bitcast.144), calls=%async_computation.6 | async-start | bytes 8388608
  443.7 9.6 %slice-start.2 = ((s8[10485760]{0:T(1024)(128)(4,1)}), s8[4194304]{0:T(1024)(128)(4,1)S(1)}, s32[]{:S(2)}) async-start(s8[10485760]{0:T(1024)(128)(4,1)} %bitcast.144), calls=%async_computation.7 | async-start | bytes 8388608
  443.7 9.9 %copy-start.1 = (bf16[1,512,1280]{1,2,0:T(8,128)(2,1)S(1)}, bf16[1,512,1280]{1,2,0:T(8,128)(2,1)}, u32[]{:S(2)}) copy-start(bf16[1,512,1280]{1,2,0:T(8,128)(2,1)} %copy.82) | copy-start | bytes 3932164
  443.7 9.9 %copy-start.5 = (pred[512,512]{0,1:T(8,128)(4,1)S(1)}, pred[512,512]{0,1:T(8,128)(4,1)}, u32[]{:S(2)}) copy-start(pred[512,512]{0,1:T(8,128)(4,1)} %copy-done.4) | copy-start | bytes 786436
  443.7 10.0 %copy-start.9 = (bf16[512,2,128]{2,1,0:T(2,128)(2,1)S(1)}, bf16[512,2,128]{2,1,0:T(2,128)(2,1)}, u32[]{:S(2)}) copy-start(bf16[512,2,128]{2,1,0:T(2,128)(2,1)} %reshape.110) | copy-start | bytes 786436
  470.8 12.1 %copy-start.3 = (bf16[1024,256]{0,1:T(8,128)(2,1)S(1)}, bf16[1024,256]{0,1:T(8,128)(2,1)}, u32[]{:S(2)}) copy-start(bf16[1024,256]{0,1:T(8,128)(2,1)} %copy.145) | copy-start | bytes 1572868
  479.6 10.5 %copy-start.2 = (bf16[1,512,1280]{1,2,0:T(8,128)(2,1)S(1)}, bf16[1,512,1280]{1,2,0:T(8,128)(2,1)}, u32[]{:S(2)}) copy-start(bf16[1,512,1280]{1,2,0:T(8,128)(2,1)} %copy.82) | copy-start | bytes 3932164
  479.6 10.5 %copy-start.6 = (pred[512,512]{0,1:T(8,128)(4,1)S(1)}, pred[512,512]{0,1:T(8,128)(4,1)}, u32[]{:S(2)}) copy-start(pred[512,512]{0,1:T(8,128)(4,1)} %copy-done.4) | copy-start | bytes 786436
  482.9 14.7 %slice-start.3 = ((s8[10485760]{0:T(1024)(128)(4,1)}), s8[4194304]{0:T(1024)(128)(4,1)S(1)}, s32[]{:S(2)}) async-start(s8[10485760]{0:T(1024)(128)(4,1)} %bitcast.146), calls=%async_computation.8 | async-start | bytes 8388608
  482.9 14.7 %slice-start.4 = ((s8[10485760]{0:T(1024)(128)(4,1)}), s8[4194304]{0:T(1024)(128)(4,1)S(1)}, s32[]{:S(2)}) async-start(s8[10485760]{0:T(1024)(128)(4,1)} %bitcast.146), calls=%async_computation.9 | async-start | bytes 8388608
  490.1 7.6 slice-start.5
  490.1 7.6 copy-start.10
  497.7 303.6 %copy-start.8 = (bf16[512,2,128,1]{0,2,3,1:T(8,128)(2,1)S(1)}, bf16[512,2,128,1]{0,2,3,1:T(8,128)(2,1)}, u32[]{:S(2)}) copy-start(bf16[512,2,128,1]{0,2,3,1:T(8,128)(2,1)} %copy-done.7) | copy-start | bytes 786436
  502.9 313.9 %copy-start.11 = (bf16[2,128,512]{2,1,0:T(8,128)(2,1)S(1)}, bf16[2,128,512]{2,1,0:T(8,128)(2,1)}, u32[]{:S(2)}) copy-start(bf16[2,128,512]{2,1,0:T(8,128)(2,1)} %fusion.21) | copy-start | bytes 786436
  774.8 31.2 %all-to-all-start = ((f32[4,8,256]{2,1,0:T(8,128)}), f32[4,8,256]{2,1,0:T(8,128)S(1)}, u32[]{:S(2)}, u32[]{:S(2)}) async-start(f32[4,8,256]{2,1,0:T(8,128)} %get-tuple-element.73), calls=%async_computation | async-start | bytes 65536 | tf_op jit(solution)/shard_map/all_to_all | solution.py:129
  806.0 14.1 %all-to-all-start.1 = ((f32[4,8,256]{2,1,0:T(8,128)}), f32[4,8,256]{2,1,0:T(8,128)S(1)}, u32[]{:S(2)}, u32[]{:S(2)}) async-start(f32[4,8,256]{2,1,0:T(8,128)} %get-tuple-element.72), calls=%async_computation.1 | async-start | bytes 65536 | tf_op jit(solution)/shard_map/all_to_all | solution.py:130
Sparse Core Ops, SparseCore 0:
  9.7 197.1 all-gather.2
  208.7 192.7 all-gather.4
  483.0 290.3 all-reduce.1
where the time goes:
time: 829 us; the launch traced here: 828 us
  waiting for transfers between devices  650 us (78%)
  matrix products  85 us (10%)
  starting transfers between devices  30.9 us (4%)
  local copies, waits for them, and re-layouts  25 us (3%)
  other arithmetic  22 us (3%)
  between operations  14.6 us (2%)
    psum x1, waiting for transfers between devices, per_device(): lax.psum(jnp.concatenate([key_part.reshape(prompt_rows, kv_width), value_...  270 us
    all_gather x1, waiting for transfers between devices, per_device(): lax.all_gather(prompt_keys, ('resp', 'head'), axis=0, tiled=True)  195 us
    all_gather x1, waiting for transfers between devices, per_device(): lax.all_gather(prompt_values, ('resp', 'head'), axis=0, tiled=True)  183 us
    all_to_all x1, starting transfers between devices, per_device(): lax.all_to_all(key_sum, 'head', split_axis=0, concat_axis=1, tiled=True)  26.5 us
  transfers between devices with their start and end apart: 5, of which 4 were waited for; matrix products, arithmetic and copies ran while one was open for 6% of the time, Pallas kernels for 0%

commit v1 on v0

--- a/solution.py
+++ b/solution.py
@@ -81,8 +81,14 @@
 ):
     kv_width = resp_keys.shape[2]
     kv_count = kv_width // HEAD_DIM
+
+    def recover_boxes(state):
+        e_now = jnp.stack([state for _ in range(lax.axis_size(("resp", "head")))])
+        later = lax.all_to_all(e_now, axis_name=("resp", "head"), split_axis=0, concat_axis=0)
+        return jnp.concatenate(later, axis=0)
+
     every_key, every_value = (
-        lax.all_gather(prompt_keys, ("resp", "head"), axis=0, tiled=True),
+        recover_boxes(prompt_keys),
         lax.all_gather(prompt_values, ("resp", "head"), axis=0, tiled=True),
     )
     head_start = lax.axis_index("head") * kv_width

time: 829 us -> 648 us (0.78)
  waiting for transfers between devices: 650 us -> 457 us
  starting transfers between devices: 30.9 us -> 42.9 us
    all_gather x1 -> x0, waiting for transfers between devices: 195 us -> none  [per_device(): lax.all_gather(prompt_keys, ('resp', 'head'), axis=0, tiled=True)]
    all_to_all x0 -> x1, waiting for transfers between devices: none -> 18.9 us  [recover_boxes(): lax.all_to_all(e_now, axis_name=('resp', 'head'), split_axis=0, concat_ax...]
    all_gather x1, waiting for transfers between devices: 183 us -> 167 us  [per_device(): lax.all_gather(prompt_values, ('resp', 'head'), axis=0, tiled=True)]
    all_to_all x0 -> x1, starting transfers between devices: none -> 12 us  [recover_boxes(): lax.all_to_all(e_now, axis_name=('resp', 'head'), split_axis=0, concat_ax...]
  transfers between devices with their start and end apart: 5 -> 5, of which waited for: 4 -> 4; matrix products, arithmetic and copies ran while one was open for 6% -> 7% of each run, Pallas kernels for 0% -> 0%
where the time goes in v1:
time: 648 us; the launch traced here: 647 us
  waiting for transfers between devices  457 us (71%)
  matrix products  85 us (13%)
  starting transfers between devices  42.9 us (7%)
  local copies, waits for them, and re-layouts  25.4 us (4%)
  other arithmetic  21.4 us (3%)
  between operations  15 us (2%)
    psum x1, waiting for transfers between devices, per_device(): lax.psum(jnp.concatenate([key_part.reshape(prompt_rows, kv_width), value_...  271 us
    all_gather x1, waiting for transfers between devices, per_device(): lax.all_gather(prompt_values, ('resp', 'head'), axis=0, tiled=True)  167 us
    all_to_all x1, starting transfers between devices, per_device(): lax.all_to_all(key_sum, 'head', split_axis=0, concat_axis=1, tiled=True)  26.5 us
    all_to_all x1, waiting for transfers between devices, recover_boxes(): lax.all_to_all(e_now, axis_name=('resp', 'head'), split_axis=0, concat_ax...  18.9 us
    reduce_sum x1, other arithmetic, respond(): row_total = jnp.exp(prompt_scores - row_top[..., None]).sum(-1) + jnp.exp...  14.2 us
    dot_general x1, matrix products, respond(): jnp.einsum('tkgd,jkd->kgtj', grad_five, prompt_value3, preferred_element_...  13 us
  transfers between devices with their start and end apart: 5, of which 4 were waited for; matrix products, arithmetic and copies ran while one was open for 7% of the time, Pallas kernels for 0%

profile of v1, /device:TPU:1, one launch (start us, length us, event | category | flops | bytes accessed | tf_op | source)
XLA Modules:
  0.0 647.1 jit_solution(5354143130701589052)
XLA Ops:
  7.9 2.3 stack.2
  10.3 12.0 %all-to-all-start = ((bf16[128,8,1024]{2,1,0:T(8,128)(2,1)}), bf16[128,8,1024]{2,1,0:T(8,128)(2,1)}, u32[]{:S(2)}, u32[]{:S(2)}) async-start(bf16[128,8,1024]{2,1,0:T(8,128)(2,1)} %stack.2), calls=%async_computation | async-start | bytes 4194304 | tf_op jit(solution)/shard_map/all_to_all | solution.py:87
  22.3 1.6 copy.74
  24.5 1.0 reshape.115
  25.8 1.5 copy.82
  28.2 6.3 fusion.11
  34.5 18.9 %all-to-all-done = bf16[128,8,1024]{2,1,0:T(8,128)(2,1)} async-done(((bf16[128,8,1024]{2,1,0:T(8,128)(2,1)}), bf16[128,8,1024]{2,1,0:T(8,128)(2,1)}, u32[]{:S(2)}, u32[]{:S(2)}) %all-to-all-start) | async-done | bytes 2097184 | tf_op jit(solution)/shard_map/all_to_all | solution.py:87
  53.4 166.7 %all-gather.2.cloned.1.call-done = bf16[1024,1024]{1,0:T(8,128)(2,1)} async-done(((bf16[8,1024]{1,0:T(8,128)(2,1)}), bf16[1024,1024]{1,0:T(8,128)(2,1)}) %all-gather.2.cloned.1.call-update) | async-done | bytes 2097168 | tf_op jit(solution)/shard_map/all_gather | solution.py:92
  220.1 2.1 constant_dynamic-slice_fusion
  223.2 4.0 bitcast_reduce_fusion
  227.2 14.2 %exponential_reduce_fusion = f32[2,5,512]{2,1,0:T(8,128)} fusion(f32[2,512,512,5]{2,1,3,0:T(8,128)} %get-tuple-element.77, f32[2,5,512]{2,1,0:T(8,128)S(1)} %max.11, pred[512,512]{0,1:T(8,128)(4,1)S(1)} %fusion.22), kind=kLoop, calls=%fused_computation.17 | loop fusion | flops 10480640 | bytes 10788864 | tf_op jit(solution)/shard_map/while/body/eval_jaxpr/reduce_sum | solution.py:32
  241.4 3.7 fusion.4
  245.2 12.4 %fusion.16 = f32[2,128,1024,1]{2,1,3,0:T(8,128)} fusion(f32[2,1024,512,5]{2,1,3,0:T(8,128)} %copy-done, f32[2,5,512]{2,1,0:T(8,128)S(1)} %log_add_fusion, bf16[512,2,5,128]{0,3,2,1:T(8,128)(2,1)} %bitcast.153, bf16[512]{0:T(512)(128)(2,1)S(1)} %select_convert_fusion), kind=kOutput, calls=%fused_computation.28 | convolution fusion | flops 1358561280 | bytes 23352320 | tf_op jit(solution)/shard_map/rkgtj,rtkgd->jkd/dot_general | solution.py:122
  257.6 2.7 copy.96
  260.3 2.0 copy.72
  262.3 9.3 %fusion.18 = f32[2,128,5,512]{3,1,2,0:T(8,128)S(1)} fusion(bf16[1024,2,128,1]{0,2,3,1:T(8,128)(2,1)} %bitcast.163, f32[2,1024,512,5]{2,1,3,0:T(8,128)} %copy-done, f32[2,5,512]{2,1,0:T(8,128)S(1)} %log_add_fusion), kind=kOutput, calls=%fused_computation.29 | convolution fusion | flops 1357905920 | bytes 24137728 | tf_op jit(solution)/shard_map/while/body/eval_jaxpr/kgtj,jkd->tkgd/dot_general | solution.py:39
  272.3 4.2 fusion.13
  276.5 13.0 %fusion.2 = bf16[2,5,512,1024]{2,3,1,0:T(8,128)(2,1)} fusion(f32[2,1024,512,5]{2,1,3,0:T(8,128)} %copy-done, f32[2,5,512]{2,1,0:T(8,128)S(1)} %get-tuple-element.78, f32[2,5,512]{2,1,0:T(8,128)S(1)} %log_add_fusion, bf16[1024,2,128,1]{0,2,3,1:T(8,128)(2,1)} %bitcast.164, bf16[512,2,5,128]{0,3,2,1:T(8,128)(2,1)} %bitcast.154, ...), kind=kOutput, calls=%fused_computation.3 | convolution fusion | flops 1376256000 | bytes 33334272 | tf_op jit(solution)/shard_map/while/body/eval_jaxpr/tkgd,jkd->kgtj/dot_general | solution.py:51
  289.4 7.5 %fusion.38 = f32[2,1024,128,1]{1,2,3,0:T(8,128)S(1)} fusion(bf16[2,5,512,1024]{2,3,1,0:T(8,128)(2,1)} %fusion.2, bf16[512,2,5,128]{0,3,2,1:T(8,128)(2,1)S(1)} %bitcast.151), kind=kOutput, calls=%fused_computation.56 | convolution fusion | flops 1342177280 | bytes 12845056 | tf_op jit(solution)/shard_map/rkgtj,rtkgd->jkd/dot_general | solution.py:119
  296.9 1.3 copy.95
  298.2 3.3 pad_maximum_fusion
  301.6 7.2 %fusion.37 = f32[2,128,5,512]{3,1,2,0:T(8,128)} fusion(bf16[1024,2,128,1]{0,2,3,1:T(8,128)(2,1)S(1)} %bitcast.160, bf16[2,5,512,1024]{2,3,1,0:T(8,128)(2,1)} %fusion.2), kind=kOutput, calls=%fused_computation.55 | convolution fusion | flops 1342177280 | bytes 13631488 | tf_op jit(solution)/shard_map/while/body/eval_jaxpr/kgtj,jkd->tkgd/dot_general | solution.py:61
  308.8 7.6 %fusion.21 = bf16[2,128,512]{2,1,0:T(8,128)(2,1)} fusion(bf16[512,2,5,128]{0,3,2,1:T(8,128)(2,1)S(1)} %bitcast.156, bf16[512]{0:T(512)(128)(2,1)S(1)} %select_convert_fusion, f32[2,512,512,5]{2,1,3,0:T(8,128)} %get-tuple-element.77, f32[2,5,512]{2,1,0:T(8,128)S(1)} %log_add_fusion, pred[512,512]{0,1:T(8,128)(4,1)S(1)} %copy-done.6), kind=kOutput, calls=%fused_computation.33 | convolution fusion | flops 682360832 | bytes 12342272 | tf_op jit(solution)/shard_map/while/body/eval_jaxpr/kgtj,tkgd->jkd/dot_general | solution.py:65
  316.4 5.2 fusion.9
  321.6 270.7 %all-reduce.2.cloned.1.call-done = f32[1024,512]{1,0:T(8,128)} async-done(((f32[1024,512]{1,0:T(8,128)}), f32[1024,512]{1,0:T(8,128)}) %all-reduce.2.cloned.1.call-update) | async-done | bytes 2097168 | tf_op jit(solution)/shard_map/psum | solution.py:125
  592.3 1.4 dynamic-slice_bitcast_fusion
  593.7 26.5 %all-to-all-start.1 = ((f32[4,8,256]{2,1,0:T(8,128)}), f32[4,8,256]{2,1,0:T(8,128)S(1)}, u32[]{:S(2)}, u32[]{:S(2)}) async-start(f32[4,8,256]{2,1,0:T(8,128)} %get-tuple-element.73), calls=%async_computation.1 | async-start | bytes 65536 | tf_op jit(solution)/shard_map/all_to_all | solution.py:135
  620.2 4.2 fusion.12
  624.9 4.3 all-to-all-start.2
  629.2 4.3 fusion.20
  633.5 1.4 copy.98
  636.6 2.4 copy.97
  (66 shorter events, 7.0 us)
Async XLA Ops:
  7.2 18.6 %copy-start.9 = (bf16[1,512,1280]{2,1,0:T(8,128)(2,1)S(1)}, bf16[1,512,1280]{2,1,0:T(8,128)(2,1)}, u32[]{:S(2)}) copy-start(bf16[1,512,1280]{2,1,0:T(8,128)(2,1)} %param.15) | copy-start | bytes 3932164
  7.2 20.1 %copy-start.10 = (bf16[1,512,256]{2,1,0:T(8,128)(2,1)S(1)}, bf16[1,512,256]{2,1,0:T(8,128)(2,1)}, u32[]{:S(2)}) copy-start(bf16[1,512,256]{2,1,0:T(8,128)(2,1)} %param.10) | copy-start | bytes 786436
  7.2 20.8 %copy-start.16 = (s32[1,512]{1,0:T(1,128)S(1)}, s32[1,512]{1,0:T(1,128)}, u32[]{:S(2)}) copy-start(s32[1,512]{1,0:T(1,128)} %param.14) | copy-start | bytes 6148
  7.2 212.9 %all-gather.2.cloned.1.call-start = ((), (), s32[]{:S(2)}) async-start(), calls=%async_computation.3 | async-start | bytes 2113536 | tf_op jit(solution)/shard_map/all_gather | solution.py:92
  10.3 43.2 %all-to-all-start = ((bf16[128,8,1024]{2,1,0:T(8,128)(2,1)}), bf16[128,8,1024]{2,1,0:T(8,128)(2,1)}, u32[]{:S(2)}, u32[]{:S(2)}) async-start(bf16[128,8,1024]{2,1,0:T(8,128)(2,1)} %stack.2), calls=%async_computation | async-start | bytes 4194304 | tf_op jit(solution)/shard_map/all_to_all | solution.py:87
  22.2 570.1 %all-reduce.2.cloned.1.call-start = ((), (), s32[]{:S(2)}) async-start(), calls=%async_computation.4 | async-start | bytes 4194304 | tf_op jit(solution)/shard_map/psum | solution.py:125
  25.8 197.4 %copy-start.7 = (bf16[512,2,128,1]{0,2,3,1:T(8,128)(2,1)}, bf16[512,2,128,1]{0,2,3,1:T(8,128)(2,1)S(1)}, u32[]{:S(2)}) copy-start(bf16[512,2,128,1]{0,2,3,1:T(8,128)(2,1)S(1)} %copy.123) | copy-start | bytes 786436
  28.2 199.0 %copy-start.4 = (pred[512,512]{0,1:T(8,128)(4,1)}, pred[512,512]{0,1:T(8,128)(4,1)S(1)}, u32[]{:S(2)}) copy-start(pred[512,512]{0,1:T(8,128)(4,1)S(1)} %fusion.22) | copy-start | bytes 786436
  223.2 4.0 copy-start.14
  227.2 17.9 %copy-start = (f32[2,1024,512,5]{2,1,3,0:T(8,128)}, f32[2,1024,512,5]{2,1,3,0:T(8,128)S(1)}, u32[]{:S(2)}) copy-start(f32[2,1024,512,5]{2,1,3,0:T(8,128)S(1)} %get-tuple-element.75) | copy-start | bytes 62914564
  241.4 3.7 copy-start.15
  257.6 14.1 %slice-start = ((s8[10485760]{0:T(1024)(128)(4,1)}), s8[2097152]{0:T(1024)(128)(4,1)S(1)}, s32[]{:S(2)}) async-start(s8[10485760]{0:T(1024)(128)(4,1)} %bitcast.145), calls=%async_computation.5 | async-start | bytes 4194304
  262.3 9.4 %slice-start.1 = ((s8[10485760]{0:T(1024)(128)(4,1)}), s8[4194304]{0:T(1024)(128)(4,1)S(1)}, s32[]{:S(2)}) async-start(s8[10485760]{0:T(1024)(128)(4,1)} %bitcast.145), calls=%async_computation.6 | async-start | bytes 8388608
  262.3 9.6 %slice-start.2 = ((s8[10485760]{0:T(1024)(128)(4,1)}), s8[4194304]{0:T(1024)(128)(4,1)S(1)}, s32[]{:S(2)}) async-start(s8[10485760]{0:T(1024)(128)(4,1)} %bitcast.145), calls=%async_computation.7 | async-start | bytes 8388608
  262.3 9.9 %copy-start.1 = (bf16[1,512,1280]{1,2,0:T(8,128)(2,1)S(1)}, bf16[1,512,1280]{1,2,0:T(8,128)(2,1)}, u32[]{:S(2)}) copy-start(bf16[1,512,1280]{1,2,0:T(8,128)(2,1)} %copy.82) | copy-start | bytes 3932164
  262.3 9.9 %copy-start.5 = (pred[512,512]{0,1:T(8,128)(4,1)S(1)}, pred[512,512]{0,1:T(8,128)(4,1)}, u32[]{:S(2)}) copy-start(pred[512,512]{0,1:T(8,128)(4,1)} %copy-done.4) | copy-start | bytes 786436
  262.3 10.0 %copy-start.11 = (bf16[512,2,128]{2,1,0:T(2,128)(2,1)S(1)}, bf16[512,2,128]{2,1,0:T(2,128)(2,1)}, u32[]{:S(2)}) copy-start(bf16[512,2,128]{2,1,0:T(2,128)(2,1)} %reshape.116) | copy-start | bytes 786436
  289.4 12.1 %copy-start.3 = (bf16[1024,256]{0,1:T(8,128)(2,1)S(1)}, bf16[1024,256]{0,1:T(8,128)(2,1)}, u32[]{:S(2)}) copy-start(bf16[1024,256]{0,1:T(8,128)(2,1)} %copy.73) | copy-start | bytes 1572868
  298.2 10.6 %copy-start.2 = (bf16[1,512,1280]{1,2,0:T(8,128)(2,1)S(1)}, bf16[1,512,1280]{1,2,0:T(8,128)(2,1)}, u32[]{:S(2)}) copy-start(bf16[1,512,1280]{1,2,0:T(8,128)(2,1)} %copy.82) | copy-start | bytes 3932164
  298.2 10.6 %copy-start.6 = (pred[512,512]{0,1:T(8,128)(4,1)S(1)}, pred[512,512]{0,1:T(8,128)(4,1)}, u32[]{:S(2)}) copy-start(pred[512,512]{0,1:T(8,128)(4,1)} %copy-done.4) | copy-start | bytes 786436
  301.6 14.8 %slice-start.3 = ((s8[10485760]{0:T(1024)(128)(4,1)}), s8[4194304]{0:T(1024)(128)(4,1)S(1)}, s32[]{:S(2)}) async-start(s8[10485760]{0:T(1024)(128)(4,1)} %bitcast.147), calls=%async_computation.8 | async-start | bytes 8388608
  301.6 14.8 %slice-start.4 = ((s8[10485760]{0:T(1024)(128)(4,1)}), s8[4194304]{0:T(1024)(128)(4,1)S(1)}, s32[]{:S(2)}) async-start(s8[10485760]{0:T(1024)(128)(4,1)} %bitcast.147), calls=%async_computation.9 | async-start | bytes 8388608
  308.8 7.6 %slice-start.5 = ((s8[10485760]{0:T(1024)(128)(4,1)}), s8[2097152]{0:T(1024)(128)(4,1)S(1)}, s32[]{:S(2)}) async-start(s8[10485760]{0:T(1024)(128)(4,1)} %bitcast.147), calls=%async_computation.10 | async-start | bytes 4194304
  308.8 7.6 %copy-start.12 = (bf16[512,2,128]{2,1,0:T(2,128)(2,1)S(1)}, bf16[512,2,128]{2,1,0:T(2,128)(2,1)}, u32[]{:S(2)}) copy-start(bf16[512,2,128]{2,1,0:T(2,128)(2,1)} %reshape.116) | copy-start | bytes 786436
  316.4 303.9 %copy-start.8 = (bf16[512,2,128,1]{0,2,3,1:T(8,128)(2,1)S(1)}, bf16[512,2,128,1]{0,2,3,1:T(8,128)(2,1)}, u32[]{:S(2)}) copy-start(bf16[512,2,128,1]{0,2,3,1:T(8,128)(2,1)} %copy-done.7) | copy-start | bytes 786436
  321.6 314.2 %copy-start.13 = (bf16[2,128,512]{2,1,0:T(8,128)(2,1)S(1)}, bf16[2,128,512]{2,1,0:T(8,128)(2,1)}, u32[]{:S(2)}) copy-start(bf16[2,128,512]{2,1,0:T(8,128)(2,1)} %fusion.21) | copy-start | bytes 786436
  593.7 31.2 %all-to-all-start.1 = ((f32[4,8,256]{2,1,0:T(8,128)}), f32[4,8,256]{2,1,0:T(8,128)S(1)}, u32[]{:S(2)}, u32[]{:S(2)}) async-start(f32[4,8,256]{2,1,0:T(8,128)} %get-tuple-element.73), calls=%async_computation.1 | async-start | bytes 65536 | tf_op jit(solution)/shard_map/all_to_all | solution.py:135
  624.9 14.2 %all-to-all-start.2 = ((f32[4,8,256]{2,1,0:T(8,128)}), f32[4,8,256]{2,1,0:T(8,128)S(1)}, u32[]{:S(2)}, u32[]{:S(2)}) async-start(f32[4,8,256]{2,1,0:T(8,128)} %get-tuple-element.72), calls=%async_computation.2 | async-start | bytes 65536 | tf_op jit(solution)/shard_map/all_to_all | solution.py:136
Sparse Core Ops, SparseCore 0:
  9.8 210.3 all-gather.1
  301.7 290.5 all-reduce.1
